TPU v7x, 256 devices: a whole 4x4x8 slice. The times are simulated.
256 devices in a mesh: inst: 8 (over y, x_lo), ax: 16 (over z, core), circ: 2 (over x_hi).
Axes of the slice: x: 4 (x_hi: 2, x_lo: 2; x = x_hi * 2 + x_lo), y: 4, z: 8, core: 2. Of those that a mesh axis runs over, the one named last changes fastest.
Arguments:
- flow_state: float32 [8, 7, 128, 128, 128], P('inst', None, 'ax', 'circ'), may hold values from -2 to 40, as said below
- thinc_flags: int32 [8, 128, 128], P('inst', 'ax', 'circ'), may hold values 0 or 1
Outputs:
- new_state: float32 [8, 7, 128, 128, 128], P('inst', None, 'ax', 'circ')
Inputs may be any that keep to these rules, and one draw needn't show every extreme that they name: `flow_state`: every cell holds a two-phase state with positive partial densities and positive pressure, whose seventh field, the volume fraction, lies between 0.02 and 0.98.
All inputs are finite; a program needn't handle non-finite values. No bound on the sum of `thinc_flags` on one device may be relied on, other than what follows from the above.
Results may differ from a plain program's by a relative error of at most 0.0003.
Values sent between devices are 32-bit elements; how exact they have to be, the bound alone decides.
No kernel may reach another device: no remote copies, remote signals or barrier semaphores. Data moves between devices by JAX's collectives and lax.ppermute only.
A program may use at most 64 MiB of HBM per device.

v0:
```python
import jax
import jax.numpy as jnp
from jax import lax
from jax.sharding import PartitionSpec as P

G_LIQ = 4.4
P_LIQ = 6.0
G_GAS = 1.4
BETA = 1.6
EPSA = 0.1
ALPHA = 4.0
DIAG0 = 0.016
OMEGA = 1.0
NU_T = 0.25


def extended(block, sides, width):
    for axis, dim in sides:
        count = lax.axis_size(axis)
        forward = [(i, i + 1) for i in range(count - 1)]
        forward.append((count - 1, 0))
        backward = [(target, source) for source, target in forward]
        low = lax.ppermute(
            lax.slice_in_dim(block, block.shape[dim] - width, None, axis=dim), axis, forward
        )
        high = lax.ppermute(lax.slice_in_dim(block, 0, width, axis=dim), axis, backward)
        block = jnp.concatenate([low, block, high], axis=dim)
    return block


def shifted(block, axis, distance):
    devices = range(lax.axis_size(axis))
    route = [((i - distance) % len(devices), i) for i in devices]
    return lax.ppermute(block, axis, route)


def from_behind(value, axis, by):
    devices = lax.axis_size(axis)
    pairs = [(i, i + by) for i in range(devices) if 0 <= i + by < devices]
    return lax.ppermute(value, axis, pairs)


def spectral_table(period_count):
    harmonic = jnp.arange(period_count, dtype=jnp.int32)
    phase_angle = jnp.pi / period_count * harmonic.astype(jnp.float32)
    sine_safe = jnp.where(harmonic == 0, 1.0, jnp.sin(phase_angle))
    parity = jnp.where(harmonic % 2 == 0, 1.0, -1.0)
    first_der = jnp.where(harmonic == 0, 0.0, 0.5 * parity * jnp.cos(phase_angle) / sine_safe)
    second = jnp.where(
        harmonic == 0,
        -(period_count * period_count + 2) / 12.0,
        -parity / (2.0 * sine_safe * sine_safe),
    )
    return OMEGA * first_der - NU_T * OMEGA * OMEGA * second


def table_lookup(table_values, instance_lag, period_count):
    harmonic = jnp.arange(period_count, dtype=jnp.int32)
    return jnp.sum(
        jnp.where(instance_lag[:, None] == harmonic[None, :], table_values[None, :], 0.0), axis=1
    )


def primitives(cells):
    density = cells[0] + cells[1]
    vel_ax = cells[2] / density
    vel_circ = cells[3] / density
    vel_rad = cells[4] / density
    fraction = cells[6]
    gamma_term = fraction / (G_LIQ - 1.0) + (1.0 - fraction) / (G_GAS - 1.0)
    stiff_term = fraction * (G_LIQ * P_LIQ / (G_LIQ - 1.0))
    kinetic = 0.5 * density * (vel_ax * vel_ax + vel_circ * vel_circ + vel_rad * vel_rad)
    pressure = (cells[5] - kinetic - stiff_term) / gamma_term
    sound_speed = jnp.sqrt(
        ((1.0 + 1.0 / gamma_term) * pressure + stiff_term / gamma_term) / density
    )
    return (density, vel_ax, vel_circ, pressure, sound_speed)


def sharpen(lower_val, centre, upper_val, offset):
    average = 0.5 * (lower_val + upper_val)
    difference = upper_val - lower_val
    steepness = 2.0 * (centre - average) / (jnp.abs(difference) + EPSA)
    return average + 0.5 * difference * jnp.tanh(BETA * (steepness + offset))


def physical(cells, fraction, circ_vel, pressure):
    return [
        cells[0] * circ_vel,
        cells[1] * circ_vel,
        cells[2] * circ_vel,
        cells[3] * circ_vel + pressure,
        cells[4] * circ_vel,
        (cells[5] + pressure) * circ_vel,
        fraction * circ_vel,
    ]


def face_flux(left_state, right_state, frac_left, frac_right):
    _, _, circ_left, press_left, sound_left = primitives(left_state)
    _, _, circ_right, press_right, sound_right = primitives(right_state)
    speed = jnp.maximum(jnp.abs(circ_left) + sound_left, jnp.abs(circ_right) + sound_right)
    flux_left = physical(left_state, frac_left, circ_left, press_left)
    flux_right = physical(right_state, frac_right, circ_right, press_right)
    jumps = [right_state[component] - left_state[component] for component in range(6)]
    jumps.append(frac_right - frac_left)
    return jnp.stack(
        [
            0.5 * (flux_left[component] + flux_right[component]) - 0.5 * speed * jumps[component]
            for component in range(7)
        ]
    )


def line_sweep(lower_coef, diagonal, upper_coef, right_side):

    def forward(carried, entries):
        ratio_prev, value_prev = carried
        below_coef, centre, above_coef, right_row = entries
        pivot_value = centre - below_coef * ratio_prev
        ratio_next = above_coef / pivot_value
        value_next = (right_row - below_coef[None] * value_prev) / pivot_value[None]
        return ((ratio_next, value_next), (ratio_next, value_next))

    start_state = (jnp.zeros_like(diagonal[0]), jnp.zeros_like(right_side[0]))
    _, (ratio_rows, value_rows) = lax.scan(
        forward, start_state, (lower_coef, diagonal, upper_coef, right_side)
    )

    def backward(following, entries):
        ratio_row, value_row = entries
        current = value_row - ratio_row[None] * following
        return (current, current)

    _, solved = lax.scan(
        backward, jnp.zeros_like(right_side[0]), (ratio_rows, value_rows), reverse=True
    )
    return solved


def local(flow_state, thinc_flags):
    own_slab = flow_state[0]
    period_count = lax.axis_size("inst")
    own_index = lax.axis_index("inst")
    table_values = spectral_table(period_count)
    portion = lax.all_gather(flow_state, "inst", axis=0, tiled=True)
    row_count = portion.shape[0]
    instance_lag = (own_index - jnp.arange(row_count, dtype=jnp.int32)) % period_count
    weights = table_lookup(table_values, instance_lag, period_count)
    spectral = jnp.sum(weights[:, None, None, None, None] * portion, axis=0)
    padded = extended(own_slab, (("circ", 2),), 2)
    circ_width = own_slab.shape[2]
    fraction = padded[6]
    flagged = (thinc_flags[0] > 0)[:, :, None]
    frac_back2 = fraction[:, 0:circ_width]
    frac_back1 = fraction[:, 1 : circ_width + 1]
    frac_here = fraction[:, 2 : circ_width + 2]
    frac_next = fraction[:, 3 : circ_width + 3]
    frac_left = jnp.where(flagged, sharpen(frac_back2, frac_back1, frac_here, 1.0), frac_back1)
    frac_right = jnp.where(flagged, sharpen(frac_back1, frac_here, frac_next, -1.0), frac_here)
    fluxes = face_flux(padded[:, :, 1 : circ_width + 1], own_slab, frac_left, frac_right)
    upper_flux = shifted(fluxes[:, :, 0:1], "circ", -1)
    residual = jnp.concatenate([fluxes[:, :, 1:], upper_flux], axis=2) - fluxes + spectral
    _, vel_ax, _, _, sound_speed = primitives(own_slab)
    radius = jnp.abs(vel_ax) + sound_speed
    coupling = -ALPHA * radius
    diagonal = DIAG0 + 2.0 * ALPHA * radius
    right_side = -residual
    field_count = own_slab.shape[0]
    ax_cells = own_slab.shape[1]
    interior = ax_cells - 1
    positions = jnp.arange(interior, dtype=jnp.int32)[:, None, None, None]
    plane_shape = (interior, 1) + radius.shape[1:]
    unit_first = jnp.broadcast_to((positions == 0).astype(jnp.float32), plane_shape)
    unit_last = jnp.broadcast_to((positions == interior - 1).astype(jnp.float32), plane_shape)
    stacked = jnp.concatenate(
        [jnp.swapaxes(right_side[:, :interior], 0, 1), unit_first, unit_last], axis=1
    )
    solved_local = line_sweep(
        coupling[:interior], diagonal[:interior], coupling[:interior], stacked
    )
    y_first = solved_local[0, :field_count]
    v_first = solved_local[0, field_count]
    w_first = solved_local[0, field_count + 1]
    y_last = solved_local[interior - 1, :field_count]
    v_last = solved_local[interior - 1, field_count]
    w_last = solved_local[interior - 1, field_count + 1]
    coup_first = coupling[0]
    coup_inner = coupling[interior - 1]
    coup_sep = coupling[ax_cells - 1]
    own_lower = -coup_sep * coup_first * v_last
    own_diag = diagonal[ax_cells - 1] - coup_sep * coup_inner * w_last
    own_rhs = right_side[:, ax_cells - 1] - coup_sep[None] * y_last
    give_first = coup_first * v_first
    give_last = coup_inner * w_first
    following = from_behind(
        jnp.concatenate([give_first[None], give_last[None], y_first], axis=0), "ax", -1
    )
    sep_rows = jnp.concatenate(
        [
            own_lower[None],
            (own_diag - coup_sep * following[0])[None],
            (-coup_sep * following[1])[None],
            own_rhs - coup_sep[None] * following[2:],
        ],
        axis=0,
    )
    gathered = lax.all_gather(sep_rows[None], "ax", axis=0, tiled=True)
    red_lower = gathered[:, 0]
    red_diag = gathered[:, 1]
    red_upper = gathered[:, 2]
    red_rhs = gathered[:, 3:]
    separators = line_sweep(red_lower, red_diag, red_upper, red_rhs)
    ax_index = lax.axis_index("ax")
    own_value = lax.dynamic_index_in_dim(separators, ax_index, 0, keepdims=False)
    prev_value = lax.dynamic_index_in_dim(
        separators, jnp.maximum(ax_index - 1, 0), 0, keepdims=False
    ) * (ax_index > 0).astype(jnp.float32)
    y_part = solved_local[:, :field_count]
    v_part = solved_local[:, field_count]
    w_part = solved_local[:, field_count + 1]
    interior_delta = (
        y_part
        - (coup_first[None] * v_part)[:, None] * prev_value[None]
        - (coup_inner[None] * w_part)[:, None] * own_value[None]
    )
    delta = jnp.swapaxes(jnp.concatenate([interior_delta, own_value[None]], axis=0), 0, 1)
    return (own_slab + delta)[None]


def solution(mesh):
    return jax.shard_map(
        local,
        mesh=mesh,
        in_specs=(P("inst", None, "ax", "circ", None), P("inst", "ax", "circ")),
        out_specs=P("inst", None, "ax", "circ", None),
        check_vma=False,
    )
```

profile of v0, /device:TPU:1, one launch (start us, length us, event | category | flops | bytes accessed | tf_op | source)
XLA Modules:
  0.0 523.3 jit_solution(5717942069486642746)
XLA Ops:
  8.1 3.6 collective-permute-start
  13.3 3.8 collective-permute-done.1
  21.8 279.9 %all-gather.4.cloned.1.call-done = f32[8,7,8,64,128]{4,3,2,1,0:T(8,128)} async-done(((f32[1,7,8,64,128]{4,3,2,1,0:T(8,128)}), f32[8,7,8,64,128]{4,3,2,1,0:T(8,128)}) %all-gather.4.cloned.1.call-update) | async-done | bytes 14680080 | tf_op jit(solution)/shard_map/all_gather | solution.py:146
  301.7 7.5 %multiply_reduce_fusion = f32[7,8,64,128]{3,2,1,0:T(8,128)S(1)} fusion(f32[8,7,8,64,128]{4,3,2,1,0:T(8,128)} %all-gather.4.cloned.1.call-done, f32[8]{0:T(128)S(1)} %select_reduce_fusion), kind=kLoop, calls=%fused_computation.25 | loop fusion | flops 6881280 | bytes 16515104 | tf_op jit(solution)/shard_map/reduce_sum | solution.py:150
  309.3 2.1 fusion.3
  315.6 16.9 %while.69 = (s32[]{:T(128)}, f32[64,128]{1,0:T(8,128)S(1)}, f32[9,64,128]{2,1,0:T(8,128)S(1)}, f32[7,64,128]{2,1,0:T(8,128)}, f32[7,9,64,128]{3,2,1,0:T(8,128)},...) while((s32[]{:T(128)}, f32[64,128]{1,0:T(8,128)S(1)}, ...), condition=%wide.region_3.4_spmd.clone, body=%wide.region_2.3_spmd.clone.sunk | while | flops 327683 | bytes 1475696 | solution.py:126
  316.2 1.8 bitcast_dynamic-update-slice_fusion.14
  318.7 1.8 bitcast_dynamic-update-slice_fusion.14
  321.1 1.8 bitcast_dynamic-update-slice_fusion.14
  323.5 1.8 bitcast_dynamic-update-slice_fusion.14
  326.0 1.8 bitcast_dynamic-update-slice_fusion.14
  328.4 1.8 bitcast_dynamic-update-slice_fusion.14
  330.8 1.8 bitcast_dynamic-update-slice_fusion.14
  334.1 18.1 %while.70 = (s32[]{:T(128)}, f32[9,64,128]{2,1,0:T(8,128)S(1)}, f32[7,9,64,128]{3,2,1,0:T(8,128)}, f32[7,9,64,128]{3,2,1,0:T(8,128)}, f32[7,64,128]{2,1,0:T(8,128)}, /*index=5*/s32[]{:T(128)}, s32[]{:T(128)}, s32[]{:T(128)}) while((s32[]{:T(128)}, f32[9,64,128]{2,1,0:T(8,128)S(1)}, f32[7,9,64,128]{3,2,1,0:T(8,128)}, ...), condition=%wide.region_5.6_spmd.clone, body=%wide.region_4.5_spmd.clone.sunk | while | flops 221188 | bytes 1278067 | solution.py:135
  334.9 1.8 bitcast_dynamic-update-slice_fusion.15
  337.5 1.8 bitcast_dynamic-update-slice_fusion.15
  340.0 1.8 bitcast_dynamic-update-slice_fusion.15
  342.6 1.8 bitcast_dynamic-update-slice_fusion.15
  345.2 1.8 bitcast_dynamic-update-slice_fusion.15
  347.7 1.8 bitcast_dynamic-update-slice_fusion.15
  350.3 1.8 bitcast_dynamic-update-slice_fusion.15
  354.0 2.7 collective-permute-start.3
  356.6 5.8 %collective-permute-done.3 = f32[9,64,128]{2,1,0:T(8,128)S(1)} collective-permute-done((f32[9,64,128]{2,1,0:T(8,128)S(1)}, f32[9,64,128]{2,1,0:T(8,128)S(1)}, u32[]{:S(2)}, u32[]{:S(2)}) %collective-permute-start.3) | collective-permute-done | bytes 294944 | tf_op jit(solution)/shard_map/ppermute | solution.py:40
  366.2 42.8 %all-gather.6.cloned.1.call-done = f32[160,64,128]{2,1,0:T(8,128)} async-done(((f32[10,64,128]{2,1,0:T(8,128)}), f32[160,64,128]{2,1,0:T(8,128)}) %all-gather.6.cloned.1.call-update) | async-done | bytes 5242896 | tf_op jit(solution)/shard_map/all_gather | solution.py:208
  409.1 4.4 slice.259
  413.4 2.5 slice_bitcast_fusion.1
  416.0 2.3 broadcast.404.clone
  418.2 49.6 %while.71 = (s32[]{:T(128)}, f32[64,128]{1,0:T(8,128)S(1)}, f32[7,64,128]{2,1,0:T(8,128)S(1)}, f32[16,64,128]{2,1,0:T(8,128)}, f32[16,7,64,128]{3,2,1,0:T(8,128)...) while((s32[]{:T(128)}, f32[64,128]{1,0:T(8,128)S(1)}, ...), condition=%wide.region_7.8_spmd.clone, body=%wide.region_6.7_spmd.clone.sunk | while | flops 262147 | bytes 1246328 | solution.py:126
  435.1 1.7 bitcast_dynamic-update-slice_fusion.17
  467.9 2.2 broadcast.404
  470.1 40.2 %while.72 = (s32[]{:T(128)}, f32[7,64,128]{2,1,0:T(8,128)S(1)}, f32[16,7,64,128]{3,2,1,0:T(8,128)}, f32[16,7,64,128]{3,2,1,0:T(8,128)}, f32[16,64,128]{2,1,0:T(8,128)}, /*index=5*/s32[]{:T(128)}, s32[]{:T(128)}, s32[]{:T(128)}) while((s32[]{:T(128)}, f32[7,64,128]{2,1,0:T(8,128)S(1)}, f32[16,7,64,128]{3,2,1,0:T(8,128)}, ...), condition=%wide.region_9.10_spmd.clone, body=%wide.region_8.9_spmd.clone.sunk | while | flops 172036 | bytes 1015923 | solution.py:135
  470.9 1.8 bitcast_dynamic-update-slice_fusion.18
  473.4 1.7 bitcast_dynamic-update-slice_fusion.18
  475.9 1.8 bitcast_dynamic-update-slice_fusion.18
  478.4 1.7 bitcast_dynamic-update-slice_fusion.18
  480.9 1.8 bitcast_dynamic-update-slice_fusion.18
  483.5 1.8 bitcast_dynamic-update-slice_fusion.18
  486.0 1.8 bitcast_dynamic-update-slice_fusion.18
  488.5 1.7 bitcast_dynamic-update-slice_fusion.18
  491.0 1.8 bitcast_dynamic-update-slice_fusion.18
  493.5 1.8 bitcast_dynamic-update-slice_fusion.18
  496.0 1.8 bitcast_dynamic-update-slice_fusion.18
  498.5 1.8 bitcast_dynamic-update-slice_fusion.18
  501.1 1.7 bitcast_dynamic-update-slice_fusion.18
  503.6 1.8 bitcast_dynamic-update-slice_fusion.18
  506.1 1.7 bitcast_dynamic-update-slice_fusion.18
  508.6 1.8 bitcast_dynamic-update-slice_fusion.18
  513.2 1.7 fusion.6
  (124 shorter events, 93.2 us)
Async XLA Ops:
  6.5 1.5 copy-start
  6.5 5.6 %copy-start.4 = (s32[1,8,64]{2,1,0:T(8,128)S(1)}, s32[1,8,64]{2,1,0:T(8,128)}, u32[]{:S(2)}) copy-start(s32[1,8,64]{2,1,0:T(8,128)} %param.11) | copy-start | bytes 6148
  6.5 295.2 %all-gather.4.cloned.1.call-start = ((), (), s32[]{:S(2)}) async-start(), calls=%async_computation | async-start | bytes 16515072 | tf_op jit(solution)/shard_map/all_gather | solution.py:146
  7.3 401.8 %all-gather.6.cloned.1.call-start = ((), (), s32[]{:S(2)}) async-start(), calls=%async_computation.1 | async-start | bytes 5570560 | tf_op jit(solution)/shard_map/all_gather | solution.py:208
  8.1 5.2 collective-permute-start
  11.7 5.3 %collective-permute-start.1 = (f32[7,8,2,128]{3,2,1,0:T(2,128)S(1)}, f32[7,8,2,128]{3,2,1,0:T(2,128)S(1)}, u32[]{:S(2)}, u32[]{:S(2)}) collective-permute-start(f32[7,8,2,128]{3,2,1,0:T(2,128)S(1)} %get-tuple-element.541), channel_id=1, source_target_pairs={{1,0},{0,1},{3,2},{2,3},{5,4},{4,5},{7,6},{6,7},{9,8},{8,9},{11,10... | collective-permute-start | bytes 172040 | tf_op jit(solution)/shard_map/ppermute | solution.py:26
  19.6 1.8 copy-start.1
  21.4 287.8 %collective-permute-start.2 = (f32[7,8,1,128]{3,2,1,0:T(1,128)S(1)}, f32[7,8,1,128]{3,2,1,0:T(1,128)S(1)}, u32[]{:S(2)}, u32[]{:S(2)}) collective-permute-start(f32[7,8,1,128]{3,2,1,0:T(1,128)S(1)} %slice.245), channel_id=1, source_target_pairs={{1,0},{0,1},{3,2},{2,3},{5,4},{4,5},{7,6},{6,7},{9,8},{8,9},{11,10... | collective-permute-start | bytes 86024 | tf_op jit(solution)/shard_map/ppermute | solution.py:34
  301.7 7.5 %copy-start.2 = (f32[7,8,64,128]{3,2,1,0:T(8,128)S(1)}, f32[7,8,64,128]{3,2,1,0:T(8,128)}, u32[]{:S(2)}) copy-start(f32[7,8,64,128]{3,2,1,0:T(8,128)} %copy-done.1) | copy-start | bytes 5505028
  311.4 1.2 copy-start.3
  354.0 8.5 %collective-permute-start.3 = (f32[9,64,128]{2,1,0:T(8,128)S(1)}, f32[9,64,128]{2,1,0:T(8,128)S(1)}, u32[]{:S(2)}, u32[]{:S(2)}) collective-permute-start(f32[9,64,128]{2,1,0:T(8,128)S(1)} %pad_maximum_fusion.4), channel_id=1, source_target_pairs={{2,0},{4,2},{6,4},{8,6},{10,8},{12,10},{14,12},{16,14},{18,16},{20... | collective-permute-start | bytes 884744 | tf_op jit(solution)/shard_map/ppermute | solution.py:40
Sparse Core Ops, SparseCore 0:
  9.1 292.5 all-gather.3
  365.2 43.7 all-gather.5
where the time goes:
time: 528 us; the launch traced here: 523 us
  waiting for transfers between devices  334 us (63%)
  other arithmetic  130 us (25%)
  local copies, waits for them, and re-layouts  38.7 us (7%)
  between operations  13.6 us (3%)
  starting transfers between devices  6.75 us (1%)
    all_gather x1, waiting for transfers between devices, local(): portion = lax.all_gather(flow_state, 'inst', axis=0, tiled=True)  280 us
    dynamic_update_slice x69, other arithmetic, line_sweep(): lax.scan(forward, start_state, (lower_coef, diagonal, upper_coef, right_s...  107 us
    all_gather x1, waiting for transfers between devices, local(): gathered = lax.all_gather(sep_rows[None], 'ax', axis=0, tiled=True)  42.8 us
    mul x23, local copies, waits for them, and re-layouts, backward(): current = value_row - ratio_row[None] * following  17.5 us
  transfers between devices with their start and end apart: 6, of which 5 were waited for; matrix products, arithmetic and copies ran while one was open for 3% of the time, Pallas kernels for 0%

commit v1 on v0

--- a/solution.py
+++ b/solution.py
@@ -205,7 +205,11 @@
         ],
         axis=0,
     )
-    gathered = lax.all_gather(sep_rows[None], "ax", axis=0, tiled=True)
+    part = sep_rows[None]
+    size = lax.axis_size("ax")
+    blocks = jnp.stack([part for _ in range(size)])
+    blocks = lax.all_to_all(blocks, "ax", split_axis=0, concat_axis=0)
+    gathered = jnp.concatenate(blocks, axis=0)
     red_lower = gathered[:, 0]
     red_diag = gathered[:, 1]
     red_upper = gathered[:, 2]

time: 528 us -> 609 us (1.15)
  waiting for transfers between devices: 334 us -> 406 us
  starting transfers between devices: 6.75 us -> 13.6 us
    all_to_all x0 -> x1, waiting for transfers between devices: none -> 115 us  [local(): blocks = lax.all_to_all(blocks, 'ax', split_axis=0, concat_axis=0)]
    all_gather x1 -> x0, waiting for transfers between devices: 42.8 us -> none  [local(): gathered = lax.all_gather(sep_rows[None], 'ax', axis=0, tiled=True)]
    all_to_all x0 -> x1, starting transfers between devices: none -> 6.87 us  [local(): blocks = lax.all_to_all(blocks, 'ax', split_axis=0, concat_axis=0)]
  transfers between devices with their start and end apart: 6 -> 6, of which waited for: 5 -> 5; matrix products, arithmetic and copies ran while one was open for 3% -> 2% of each run, Pallas kernels for 0% -> 0%
where the time goes in v1:
time: 609 us; the launch traced here: 605 us
  waiting for transfers between devices  406 us (67%)
  other arithmetic  130 us (21%)
  local copies, waits for them, and re-layouts  41.8 us (7%)
  starting transfers between devices  13.6 us (2%)
  between operations  13.6 us (2%)
    all_gather x1, waiting for transfers between devices, local(): portion = lax.all_gather(flow_state, 'inst', axis=0, tiled=True)  280 us
    all_to_all x1, waiting for transfers between devices, local(): blocks = lax.all_to_all(blocks, 'ax', split_axis=0, concat_axis=0)  115 us
    dynamic_update_slice x69, other arithmetic, line_sweep(): lax.scan(forward, start_state, (lower_coef, diagonal, upper_coef, right_s...  108 us
    mul x23, local copies, waits for them, and re-layouts, backward(): current = value_row - ratio_row[None] * following  17.5 us
  transfers between devices with their start and end apart: 6, of which 5 were waited for; matrix products, arithmetic and copies ran while one was open for 2% of the time, Pallas kernels for 0%

profile of v1, /device:TPU:1, one launch (start us, length us, event | category | flops | bytes accessed | tf_op | source)
XLA Modules:
  0.0 604.8 jit_solution(7769474732519094724)
XLA Ops:
  8.1 3.6 collective-permute-start
  13.3 3.8 collective-permute-done.1
  21.8 279.9 %all-gather.2.cloned.1.call-done = f32[8,7,8,64,128]{4,3,2,1,0:T(8,128)} async-done(((f32[1,7,8,64,128]{4,3,2,1,0:T(8,128)}), f32[8,7,8,64,128]{4,3,2,1,0:T(8,128)}) %all-gather.2.cloned.1.call-update) | async-done | bytes 14680080 | tf_op jit(solution)/shard_map/all_gather | solution.py:146
  301.7 7.5 %multiply_reduce_fusion = f32[7,8,64,128]{3,2,1,0:T(8,128)S(1)} fusion(f32[8,7,8,64,128]{4,3,2,1,0:T(8,128)} %all-gather.2.cloned.1.call-done, f32[8]{0:T(128)S(1)} %select_reduce_fusion), kind=kLoop, calls=%fused_computation.25 | loop fusion | flops 6881280 | bytes 16515104 | tf_op jit(solution)/shard_map/reduce_sum | solution.py:150
  309.3 2.1 fusion.3
  315.6 17.0 %while.69 = (s32[]{:T(128)}, f32[64,128]{1,0:T(8,128)S(1)}, f32[9,64,128]{2,1,0:T(8,128)S(1)}, f32[7,64,128]{2,1,0:T(8,128)}, f32[7,9,64,128]{3,2,1,0:T(8,128)},...) while((s32[]{:T(128)}, f32[64,128]{1,0:T(8,128)S(1)}, ...), condition=%wide.region_3.4_spmd.clone, body=%wide.region_2.3_spmd.clone.sunk | while | flops 327683 | bytes 1475696 | solution.py:126
  316.3 1.8 bitcast_dynamic-update-slice_fusion.14
  318.7 1.8 bitcast_dynamic-update-slice_fusion.14
  321.1 1.8 bitcast_dynamic-update-slice_fusion.14
  323.6 1.8 bitcast_dynamic-update-slice_fusion.14
  326.0 1.8 bitcast_dynamic-update-slice_fusion.14
  328.4 1.8 bitcast_dynamic-update-slice_fusion.14
  330.8 1.8 bitcast_dynamic-update-slice_fusion.14
  334.2 18.1 %while.70 = (s32[]{:T(128)}, f32[9,64,128]{2,1,0:T(8,128)S(1)}, f32[7,9,64,128]{3,2,1,0:T(8,128)}, f32[7,9,64,128]{3,2,1,0:T(8,128)}, f32[7,64,128]{2,1,0:T(8,128)}, /*index=5*/s32[]{:T(128)}, s32[]{:T(128)}, s32[]{:T(128)}) while((s32[]{:T(128)}, f32[9,64,128]{2,1,0:T(8,128)S(1)}, f32[7,9,64,128]{3,2,1,0:T(8,128)}, ...), condition=%wide.region_5.6_spmd.clone, body=%wide.region_4.5_spmd.clone.sunk | while | flops 221188 | bytes 1278067 | solution.py:135
  335.0 1.8 bitcast_dynamic-update-slice_fusion.15
  337.6 1.8 bitcast_dynamic-update-slice_fusion.15
  340.1 1.8 bitcast_dynamic-update-slice_fusion.15
  342.7 1.8 bitcast_dynamic-update-slice_fusion.15
  345.3 1.8 bitcast_dynamic-update-slice_fusion.15
  347.9 1.8 bitcast_dynamic-update-slice_fusion.15
  350.5 1.8 bitcast_dynamic-update-slice_fusion.15
  354.1 2.7 collective-permute-start.3
  356.8 5.8 collective-permute-done.3
  364.5 3.0 stack.8
  367.5 6.9 %all-to-all-start = ((f32[16,1,10,64,128]{4,3,2,1,0:T(8,128)}), f32[16,1,10,64,128]{4,3,2,1,0:T(8,128)}, u32[]{:S(2)}, u32[]{:S(2)}) async-start(f32[16,1,10,64,128]{4,3,2,1,0:T(8,128)} %stack.8), calls=%async_computation | async-start | bytes 10485760 | tf_op jit(solution)/shard_map/all_to_all | solution.py:211
  375.6 114.8 %all-to-all-done = f32[16,1,10,64,128]{4,3,2,1,0:T(8,128)} async-done(((f32[16,1,10,64,128]{4,3,2,1,0:T(8,128)}), f32[16,1,10,64,128]{4,3,2,1,0:T(8,128)}, u32[]{:S(2)}, u32[]{:S(2)}) %all-to-all-start) | async-done | bytes 5242912 | tf_op jit(solution)/shard_map/all_to_all | solution.py:211
  490.4 4.4 slice.259
  494.8 2.5 slice_bitcast_fusion.1
  497.3 2.3 broadcast.406.clone
  499.6 49.7 %while.71 = (s32[]{:T(128)}, f32[64,128]{1,0:T(8,128)S(1)}, f32[7,64,128]{2,1,0:T(8,128)S(1)}, f32[16,64,128]{2,1,0:T(8,128)}, f32[16,7,64,128]{3,2,1,0:T(8,128)...) while((s32[]{:T(128)}, f32[64,128]{1,0:T(8,128)S(1)}, ...), condition=%wide.region_7.8_spmd.clone, body=%wide.region_6.7_spmd.clone.sunk | while | flops 262147 | bytes 1246328 | solution.py:126
  549.3 2.3 broadcast.406
  551.5 40.3 %while.72 = (s32[]{:T(128)}, f32[7,64,128]{2,1,0:T(8,128)S(1)}, f32[16,7,64,128]{3,2,1,0:T(8,128)}, f32[16,7,64,128]{3,2,1,0:T(8,128)}, f32[16,64,128]{2,1,0:T(8,128)}, /*index=5*/s32[]{:T(128)}, s32[]{:T(128)}, s32[]{:T(128)}) while((s32[]{:T(128)}, f32[7,64,128]{2,1,0:T(8,128)S(1)}, f32[16,7,64,128]{3,2,1,0:T(8,128)}, ...), condition=%wide.region_9.10_spmd.clone, body=%wide.region_8.9_spmd.clone.sunk | while | flops 172036 | bytes 1015923 | solution.py:135
  552.3 1.8 bitcast_dynamic-update-slice_fusion.18
  554.8 1.8 bitcast_dynamic-update-slice_fusion.18
  557.3 1.7 bitcast_dynamic-update-slice_fusion.18
  559.8 1.8 bitcast_dynamic-update-slice_fusion.18
  562.3 1.8 bitcast_dynamic-update-slice_fusion.18
  564.9 1.7 bitcast_dynamic-update-slice_fusion.18
  567.4 1.8 bitcast_dynamic-update-slice_fusion.18
  569.9 1.7 bitcast_dynamic-update-slice_fusion.18
  572.4 1.8 bitcast_dynamic-update-slice_fusion.18
  574.9 1.8 bitcast_dynamic-update-slice_fusion.18
  577.5 1.8 bitcast_dynamic-update-slice_fusion.18
  580.0 1.8 bitcast_dynamic-update-slice_fusion.18
  582.5 1.7 bitcast_dynamic-update-slice_fusion.18
  585.0 1.8 bitcast_dynamic-update-slice_fusion.18
  587.5 1.8 bitcast_dynamic-update-slice_fusion.18
  590.0 1.8 bitcast_dynamic-update-slice_fusion.18
  (124 shorter events, 96.1 us)
Async XLA Ops:
  6.5 1.5 copy-start
  6.5 5.6 copy-start.4
  6.5 295.2 %all-gather.2.cloned.1.call-start = ((), (), s32[]{:S(2)}) async-start(), calls=%async_computation.1 | async-start | bytes 16515072 | tf_op jit(solution)/shard_map/all_gather | solution.py:146
  8.1 5.2 collective-permute-start
  11.7 5.3 collective-permute-start.1
  19.6 1.8 copy-start.1
  21.4 287.8 %collective-permute-start.2 = (f32[7,8,1,128]{3,2,1,0:T(1,128)S(1)}, f32[7,8,1,128]{3,2,1,0:T(1,128)S(1)}, u32[]{:S(2)}, u32[]{:S(2)}) collective-permute-start(f32[7,8,1,128]{3,2,1,0:T(1,128)S(1)} %slice.245), channel_id=1, source_target_pairs={{1,0},{0,1},{3,2},{2,3},{5,4},{4,5},{7,6},{6,7},{9,8},{8,9},{11,10... | collective-permute-start | bytes 86024 | tf_op jit(solution)/shard_map/ppermute | solution.py:34
  301.7 7.5 %copy-start.2 = (f32[7,8,64,128]{3,2,1,0:T(8,128)S(1)}, f32[7,8,64,128]{3,2,1,0:T(8,128)}, u32[]{:S(2)}) copy-start(f32[7,8,64,128]{3,2,1,0:T(8,128)} %copy-done.1) | copy-start | bytes 5505028
  311.4 1.2 copy-start.3
  354.1 8.5 %collective-permute-start.3 = (f32[9,64,128]{2,1,0:T(8,128)S(1)}, f32[9,64,128]{2,1,0:T(8,128)S(1)}, u32[]{:S(2)}, u32[]{:S(2)}) collective-permute-start(f32[9,64,128]{2,1,0:T(8,128)S(1)} %pad_maximum_fusion.4), channel_id=1, source_target_pairs={{2,0},{4,2},{6,4},{8,6},{10,8},{12,10},{14,12},{16,14},{18,16},{20... | collective-permute-start | bytes 884744 | tf_op jit(solution)/shard_map/ppermute | solution.py:40
  367.5 122.9 %all-to-all-start = ((f32[16,1,10,64,128]{4,3,2,1,0:T(8,128)}), f32[16,1,10,64,128]{4,3,2,1,0:T(8,128)}, u32[]{:S(2)}, u32[]{:S(2)}) async-start(f32[16,1,10,64,128]{4,3,2,1,0:T(8,128)} %stack.8), calls=%async_computation | async-start | bytes 10485760 | tf_op jit(solution)/shard_map/all_to_all | solution.py:211
Sparse Core Ops, SparseCore 0:
  9.1 292.5 all-gather.1
